TPU v7x, 512 devices: a whole 4x4x16 slice. The times are simulated.
512 devices in a mesh: db: 64 (over z, x), seq: 8 (over y, core).
Axes of the slice: x: 4, y: 4, z: 16, core: 2. Of those that a mesh axis runs over, the one named last changes fastest.
Arguments:
- reader: bfloat16 [64, 1024, 2048], P('db', 'seq'), may hold values from -6 to 6
- reader_gain: float32 [2048], replicated, may hold values from 0.1 to 1.9
- database: bfloat16 [8192, 2, 896], P('db')
- encoder_gain: float32 [896], replicated, may hold values from 0.1 to 1.9
- w_expand: bfloat16 [896, 1792], P('db', 'seq'), may hold values from -0.1875 to 0.1875
- w_reduce: bfloat16 [1792, 896], P('seq', 'db'), may hold values from -0.125 to 0.125
- w_query: bfloat16 [2048, 2048], P('db', 'seq'), may hold values from -0.125 to 0.125
- w_key: bfloat16 [896, 2048], P('db', 'seq'), may hold values from -0.1875 to 0.1875
- w_value: bfloat16 [896, 2048], P('db', 'seq'), may hold values from -0.1875 to 0.1875
- w_output: bfloat16 [2048, 2048], P('db', 'seq'), may hold values from -0.125 to 0.125
- neighbour_ids: int32 [64, 8, 4], replicated, may hold values from 0 to 127
- lengths: int32 [64, 8, 4], P('db'), may hold values from 1 to 128, 320 in all within a row
- owners: int32 [64, 8, 4], P('db'), may hold values from 0 to 63
Outputs:
- updated: bfloat16 [64, 1024, 2048], P('db', None, 'seq')
Inputs may be any that keep to these rules, and one draw needn't show every extreme that they name: For every sequence b and every q, the lengths[b, q, :] of its 4 neighbours sum to exactly 320, and the longest of them is 128.
All inputs are finite; a program needn't handle non-finite values.
Results may differ from a plain program's by a relative error of at most 0.0065.
The roundings to bfloat16 on the way count: a program that leaves them out, or rounds other values in their place, can miss the bound.
Values may be sent and summed in bfloat16 or wider, within the bound.
No kernel may reach another device: no remote copies, remote signals or barrier semaphores. Data moves between devices by JAX's collectives and lax.ppermute only.
A program may use at most 64 MiB of HBM per device.

v0:
```python
import jax
import jax.numpy as jnp
from jax import lax
from jax.sharding import PartitionSpec as P

HD = 128
SPAN = 64
KNN = 2
epsilon = 1e-06


def rms_scale(values, scales):
    widened = values.astype(jnp.float32)
    mean_square = jnp.mean(widened * widened, axis=-1, keepdims=True)
    return widened * lax.rsqrt(mean_square + epsilon) * scales


def body(
    reader,
    reader_gain,
    database,
    encoder_gain,
    w_expand,
    w_reduce,
    w_query,
    w_key,
    w_value,
    w_output,
    neighbour_ids,
    lengths,
    owners,
):
    shards = lax.axis_size("db")
    seq_index = lax.axis_index("seq")
    entries, stripe, features = database.shape
    query_part = lax.all_gather(w_query, "db", axis=0, tiled=True)
    reader_output_part = lax.all_gather(w_output, "db", axis=0, tiled=True)
    rows = lax.all_gather(reader[0], "seq", axis=0, tiled=True)
    normed_tokens = rms_scale(rows, reader_gain).astype(jnp.bfloat16)
    queries = jnp.dot(normed_tokens, query_part, preferred_element_type=jnp.float32).astype(
        jnp.bfloat16
    )
    rows, queries, output_part = (rows, queries, reader_output_part)
    expand_part = lax.all_gather(w_expand, "db", axis=0, tiled=True)
    reduce_part = lax.all_gather(w_reduce, "db", axis=1, tiled=True)
    key_part = lax.all_gather(w_key, "db", axis=0, tiled=True)
    value_part = lax.all_gather(w_value, "db", axis=0, tiled=True)
    stored = database.reshape(entries * stripe, features)
    normed_rows = rms_scale(stored, encoder_gain).astype(jnp.bfloat16)
    hidden = jax.nn.gelu(
        jnp.dot(normed_rows, expand_part, preferred_element_type=jnp.float32), approximate=False
    ).astype(jnp.bfloat16)
    partial_sum = jnp.dot(hidden, reduce_part, preferred_element_type=jnp.float32)
    total = lax.psum(partial_sum, "seq")
    encoded = (stored.astype(jnp.float32) + total).astype(jnp.bfloat16)
    w_pairs = jnp.concatenate([key_part, value_part], axis=1)
    table = jnp.dot(encoded, w_pairs, preferred_element_type=jnp.float32).astype(jnp.bfloat16)
    table = table.reshape(entries, stripe, w_pairs.shape[1])
    requests = neighbour_ids.reshape(shards, -1)
    outgoing = table[requests]
    arrived = lax.all_to_all(outgoing, "db", split_axis=0, concat_axis=0, tiled=True)
    seq_len = rows.shape[0]
    per_seq = neighbour_ids.shape[1] * neighbour_ids.shape[2]
    width = arrived.shape[-1]
    local_heads = width // (2 * HD)
    positions = jnp.arange(stripe * shards, dtype=jnp.int32)
    owner_flat = owners[0].reshape(-1)
    length_flat = lengths[0].reshape(-1)
    source = (owner_flat[:, None] + positions[None, :] // stripe) % shards
    neighbour_index = jnp.arange(per_seq, dtype=jnp.int32)[:, None]
    flat_index = (source * per_seq + neighbour_index) * stripe + (positions % stripe)[None, :]
    key_value = arrived.reshape(-1, width)[flat_index]
    live = positions[None, :] < length_flat[:, None]
    spans = per_seq // KNN
    window = KNN * positions.shape[0]
    span_pairs = key_value.reshape(spans, window, width)
    span_live = live.reshape(spans, window)
    prior_pairs = jnp.concatenate(
        [jnp.zeros((1, window, width), jnp.bfloat16), span_pairs[:-1]], axis=0
    )
    prior_live = jnp.concatenate([jnp.zeros((1, window), bool), span_live[:-1]], axis=0)
    query_spans = queries.reshape(spans, SPAN, local_heads, HD)
    key_heads = prior_pairs[:, :, : local_heads * HD].reshape(spans, window, local_heads, HD)
    value_heads = prior_pairs[:, :, local_heads * HD :].reshape(spans, window, local_heads, HD)
    scores = jnp.einsum(
        "cqhd,ckhd->chqk", query_spans, key_heads, preferred_element_type=jnp.float32
    ) * HD ** (-0.5)
    masked = jnp.where(prior_live[:, None, None, :], scores, -jnp.inf)
    largest = jnp.max(masked, axis=-1, keepdims=True)
    largest = jnp.where(jnp.isfinite(largest), largest, 0.0)
    powers = jnp.exp(masked - largest)
    totals = jnp.sum(powers, axis=-1, keepdims=True)
    weights = (powers / jnp.where(totals > 0, totals, 1.0)).astype(jnp.bfloat16)
    attended = jnp.einsum(
        "chqk,ckhd->cqhd", weights, value_heads, preferred_element_type=jnp.float32
    )
    attended = attended.reshape(seq_len, local_heads * HD).astype(jnp.bfloat16)
    model_cols = output_part.shape[1]
    update = jnp.dot(
        lax.all_gather(attended, "seq", axis=1, tiled=True),
        output_part,
        preferred_element_type=jnp.float32,
    )
    residual = lax.dynamic_slice_in_dim(rows, seq_index * model_cols, model_cols, 1)
    result = (residual.astype(jnp.float32) + update).astype(jnp.bfloat16)
    return result[None]


def solution(mesh):
    in_specs = (
        P("db", "seq", None),
        P(),
        P("db", None, None),
        P(),
        P("db", "seq"),
        P("seq", "db"),
        P("db", "seq"),
        P("db", "seq"),
        P("db", "seq"),
        P("db", "seq"),
        P(),
        P("db", None, None),
        P("db", None, None),
    )
    out_specs = P("db", None, "seq")
    return jax.shard_map(body, mesh=mesh, in_specs=in_specs, out_specs=out_specs, check_vma=False)
```

profile of v0, /device:TPU:1, one launch (start us, length us, event | category | flops | bytes accessed | tf_op | source)
XLA Modules:
  0.0 866.5 jit_solution(5057858195962454341)
XLA Ops:
  6.5 1.2 reshape.275
  7.7 1.6 multiply_reduce_fusion
  9.3 81.7 %all-gather.2 = bf16[64,14,224]{2,1,0:T(8,128)(2,1)S(1)} all-gather(bf16[1,14,224]{2,1,0:T(8,128)(2,1)} %bitcast.53), channel_id=1, replica_groups=mesh['db'=64,'seq'=8] {'db'}, dimensions={0}, use_global_device_ids=true | all-gather | bytes 407680 | tf_op jit(solution)/shard_map/all_gather | solution.py:45
  91.2 73.5 %all-gather.1 = bf16[64,14,224]{2,1,0:T(8,128)(2,1)S(1)} all-gather(bf16[1,14,224]{2,1,0:T(8,128)(2,1)S(1)} %bitcast.54), channel_id=1, replica_groups=mesh['db'=64,'seq'=8] {'db'}, dimensions={0}, use_global_device_ids=true | all-gather | bytes 407680 | tf_op jit(solution)/shard_map/all_gather | solution.py:44
  165.1 2.4 fusion.38
  167.5 73.3 %all-gather.4 = bf16[64,14,256]{2,1,0:T(8,128)(2,1)S(1)} all-gather(bf16[1,14,256]{2,1,0:T(8,128)(2,1)S(1)} %bitcast.55), channel_id=1, replica_groups=mesh['db'=64,'seq'=8] {'db'}, dimensions={0}, use_global_device_ids=true | all-gather | bytes 465920 | tf_op jit(solution)/shard_map/all_gather | solution.py:47
  240.8 75.0 %all-gather.3 = bf16[64,14,256]{2,1,0:T(8,128)(2,1)S(1)} all-gather(bf16[1,14,256]{2,1,0:T(8,128)(2,1)S(1)} %bitcast.56), channel_id=1, replica_groups=mesh['db'=64,'seq'=8] {'db'}, dimensions={0}, use_global_device_ids=true | all-gather | bytes 465920 | tf_op jit(solution)/shard_map/all_gather | solution.py:46
  316.3 1.6 convolution_convert_fusion.1
  318.1 21.4 %gather_fusion = bf16[2048,2,512]{2,1,0:T(2,128)(2,1)} fusion(bf16[128,2,512]{2,1,0:T(2,128)(2,1)S(1)} %reshape.269, s32[2048]{0:T(1024)S(1)} %broadcast_clamp_fusion), kind=kCustom, calls=%fused_computation | custom fusion | bytes 8396800 | tf_op jit(solution)/shard_map/gather | solution.py:60
  339.5 10.5 %all-to-all-start = ((bf16[64,32,2,512]{3,2,1,0:T(2,128)(2,1)}), bf16[64,32,2,512]{3,2,1,0:T(2,128)(2,1)}, u32[]{:S(2)}, u32[]{:S(2)}) async-start(bf16[64,32,2,512]{3,2,1,0:T(2,128)(2,1)} %bitcast.46), calls=%async_computation | async-start | bytes 8388608 | tf_op jit(solution)/shard_map/all_to_all | solution.py:61
  352.8 174.3 %all-gather.16.cloned.1.call-done = bf16[1,1024,2048]{2,1,0:T(8,128)(2,1)} async-done(((bf16[1,128,2048]{2,1,0:T(8,128)(2,1)}), bf16[1,1024,2048]{2,1,0:T(8,128)(2,1)}) %all-gather.16.cloned.1.call-update) | async-done | bytes 4194320 | tf_op jit(solution)/shard_map/all_gather | solution.py:38
  527.1 3.1 fusion
  530.2 134.5 %all-gather.10.cloned.1.call-done = bf16[2048,256]{1,0:T(8,128)(2,1)} async-done(((bf16[32,256]{1,0:T(8,128)(2,1)}), bf16[2048,256]{1,0:T(8,128)(2,1)}) %all-gather.10.cloned.1.call-update) | async-done | bytes 1048592 | tf_op jit(solution)/shard_map/all_gather | solution.py:36
  664.7 3.8 fusion.11
  668.6 7.2 reshape.271
  675.8 20.1 %gather_fusion.1 = bf16[4096,512]{1,0:T(8,128)(2,1)} fusion(bf16[4096,512]{1,0:T(8,128)(2,1)} %reshape.271, s32[4096]{0:T(1024)S(1)} %fusion.75), kind=kCustom, calls=%fused_computation.1 | custom fusion | bytes 8404992 | tf_op jit(solution)/shard_map/gather | solution.py:72
  695.9 4.2 slice.29
  700.2 6.3 copy.31
  706.4 2.6 pad_slice_fusion
  709.7 0.9 fusion.9
  710.6 1.0 fusion.14
  713.1 90.4 %all-gather.14.cloned.1.call-done = bf16[2048,256]{1,0:T(8,128)(2,1)} async-done(((bf16[32,256]{1,0:T(8,128)(2,1)}), bf16[2048,256]{1,0:T(8,128)(2,1)}) %all-gather.14.cloned.1.call-update) | async-done | bytes 1048592 | tf_op jit(solution)/shard_map/all_gather | solution.py:37
  803.5 51.9 %all-gather.12.cloned.1.call-done = bf16[1024,2048]{1,0:T(8,128)(2,1)} async-done(((bf16[1024,256]{1,0:T(8,128)(2,1)}), bf16[1024,2048]{1,0:T(8,128)(2,1)}) %all-gather.12.cloned.1.call-update) | async-done | bytes 4194320 | tf_op jit(solution)/shard_map/all_gather | solution.py:100
  855.3 4.6 fusion.15
  (55 shorter events, 6.2 us)
Async XLA Ops:
  6.5 84.7 %copy-start.1 = (bf16[14,224]{1,0:T(8,128)(2,1)S(1)}, bf16[14,224]{1,0:T(8,128)(2,1)}, u32[]{:S(2)}) copy-start(bf16[14,224]{1,0:T(8,128)(2,1)} %param.17) | copy-start | bytes 18820
  6.5 309.8 %all-reduce.4.cloned.1.call-start = ((), (), s32[]{:S(2)}) async-start(), calls=%async_computation.1 | async-start | bytes 1835008 | tf_op jit(solution)/shard_map/psum | solution.py:54
  7.7 157.4 %copy-start.7 = (f32[896]{0:T(1024)S(1)}, f32[896]{0:T(1024)}, u32[]{:S(2)}) copy-start(f32[896]{0:T(1024)} %param.16) | copy-start | bytes 10756
  165.1 2.4 copy-start.2
  165.1 75.7 %copy-start.3 = (bf16[14,256]{1,0:T(8,128)(2,1)S(1)}, bf16[14,256]{1,0:T(8,128)(2,1)}, u32[]{:S(2)}) copy-start(bf16[14,256]{1,0:T(8,128)(2,1)} %param.20) | copy-start | bytes 21508
  167.5 148.6 %copy-start = (s32[64,8,4]{0,2,1:T(4,128)S(1)}, s32[64,8,4]{0,2,1:T(4,128)}, u32[]{:S(2)}) copy-start(s32[64,8,4]{0,2,1:T(4,128)} %param.23) | copy-start | bytes 24580
  339.5 12.8 %copy-start.4 = (s32[1,8,4]{1,2,0:T(4,128)S(1)}, s32[1,8,4]{1,2,0:T(4,128)}, u32[]{:S(2)}) copy-start(s32[1,8,4]{1,2,0:T(4,128)} %param.25) | copy-start | bytes 388
  339.5 12.9 %copy-start.5 = (s32[1,8,4]{1,2,0:T(4,128)S(1)}, s32[1,8,4]{1,2,0:T(4,128)}, u32[]{:S(2)}) copy-start(s32[1,8,4]{1,2,0:T(4,128)} %param.24) | copy-start | bytes 388
  339.5 329.1 %all-to-all-start = ((bf16[64,32,2,512]{3,2,1,0:T(2,128)(2,1)}), bf16[64,32,2,512]{3,2,1,0:T(2,128)(2,1)}, u32[]{:S(2)}, u32[]{:S(2)}) async-start(bf16[64,32,2,512]{3,2,1,0:T(2,128)(2,1)} %bitcast.46), calls=%async_computation | async-start | bytes 8388608 | tf_op jit(solution)/shard_map/all_to_all | solution.py:61
  349.9 177.2 %all-gather.16.cloned.1.call-start = ((), (), s32[]{:S(2)}) async-start(), calls=%async_computation.5 | async-start | bytes 4718592 | tf_op jit(solution)/shard_map/all_gather | solution.py:38
  350.7 314.0 %all-gather.10.cloned.1.call-start = ((), (), s32[]{:S(2)}) async-start(), calls=%async_computation.2 | async-start | bytes 1064960 | tf_op jit(solution)/shard_map/all_gather | solution.py:36
  351.4 452.0 %all-gather.14.cloned.1.call-start = ((), (), s32[]{:S(2)}) async-start(), calls=%async_computation.4 | async-start | bytes 1064960 | tf_op jit(solution)/shard_map/all_gather | solution.py:37
  352.0 503.3 %all-gather.12.cloned.1.call-start = ((), (), s32[]{:S(2)}) async-start(), calls=%async_computation.3 | async-start | bytes 4718592 | tf_op jit(solution)/shard_map/all_gather | solution.py:100
  352.8 311.9 %copy-start.6 = (f32[2048]{0:T(1024)S(1)}, f32[2048]{0:T(1024)}, u32[]{:S(2)}) copy-start(f32[2048]{0:T(1024)} %param.14) | copy-start | bytes 24580
Sparse Core Ops, SparseCore 0:
  167.7 123.3 all-reduce.3
  352.9 174.1 all-gather.15
  530.1 134.5 all-gather.9
  667.5 135.9 all-gather.13
  805.4 49.8 all-gather.11
where the time goes:
time: 867 us; the launch traced here: 866 us
  waiting for transfers between devices  453 us (52%)
  blocking collectives  303 us (35%)
  local copies, waits for them, and re-layouts  66 us (8%)
  matrix products  14 us (2%)
  between operations  13.4 us (2%)
  starting transfers between devices  10.8 us (1%)
    all_gather x1, waiting for transfers between devices, body(): rows = lax.all_gather(reader[0], 'seq', axis=0, tiled=True)  174 us
    all_gather x1, waiting for transfers between devices, body(): query_part = lax.all_gather(w_query, 'db', axis=0, tiled=True)  134 us
    all_gather x1, waiting for transfers between devices, body(): reader_output_part = lax.all_gather(w_output, 'db', axis=0, tiled=True)  90.4 us
    all_gather x1, blocking collectives, body(): reduce_part = lax.all_gather(w_reduce, 'db', axis=1, tiled=True)  81.7 us
    all_gather x1, blocking collectives, body(): key_part = lax.all_gather(w_key, 'db', axis=0, tiled=True)  75 us
    all_gather x1, blocking collectives, body(): expand_part = lax.all_gather(w_expand, 'db', axis=0, tiled=True)  73.5 us
    all_gather x1, blocking collectives, body(): value_part = lax.all_gather(w_value, 'db', axis=0, tiled=True)  73.3 us
    all_gather x1, waiting for transfers between devices, body(): lax.all_gather(attended, 'seq', axis=1, tiled=True)  51.9 us
  transfers between devices with their start and end apart: 6, of which 4 were waited for; matrix products, arithmetic and copies ran while one was open for 6% of the time, Pallas kernels for 0%

commit v1 on v0

--- a/solution.py
+++ b/solution.py
@@ -33,7 +33,9 @@
     shards = lax.axis_size("db")
     seq_index = lax.axis_index("seq")
     entries, stripe, features = database.shape
-    query_part = lax.all_gather(w_query, "db", axis=0, tiled=True)
+    query_part = jnp.concatenate(
+        lax.all_to_all(jnp.stack([w_query] * lax.axis_size("db")), "db", 0, 0), axis=0
+    )
     reader_output_part = lax.all_gather(w_output, "db", axis=0, tiled=True)
     rows = lax.all_gather(reader[0], "seq", axis=0, tiled=True)
     normed_tokens = rms_scale(rows, reader_gain).astype(jnp.bfloat16)

time: 867 us -> 788 us (0.909)
  waiting for transfers between devices: 453 us -> 318 us
  blocking collectives: 303 us -> 338 us
  starting transfers between devices: 10.8 us -> 31.2 us
    all_gather x1 -> x0, waiting for transfers between devices: 134 us -> none  [body(): query_part = lax.all_gather(w_query, 'db', axis=0, tiled=True)]
    all_gather x1, blocking collectives: 81.7 us -> 116 us  [body(): reduce_part = lax.all_gather(w_reduce, 'db', axis=1, tiled=True)]
    all_to_all x0 -> x1, starting transfers between devices: none -> 19.2 us  [body(): lax.all_to_all(jnp.stack([w_query] * lax.axis_size('db')), 'db', 0, 0)]
  transfers between devices with their start and end apart: 6 -> 6, of which waited for: 4 -> 3; matrix products, arithmetic and copies ran while one was open for 6% -> 10% of each run, Pallas kernels for 0% -> 0%
where the time goes in v1:
time: 788 us; the launch traced here: 787 us
  blocking collectives  338 us (43%)
  waiting for transfers between devices  318 us (40%)
  local copies, waits for them, and re-layouts  67.9 us (9%)
  starting transfers between devices  31.2 us (4%)
  between operations  13.4 us (2%)
  matrix products  12.5 us (2%)
    all_gather x1, waiting for transfers between devices, body(): rows = lax.all_gather(reader[0], 'seq', axis=0, tiled=True)  177 us
    all_gather x1, blocking collectives, body(): reduce_part = lax.all_gather(w_reduce, 'db', axis=1, tiled=True)  116 us
    all_gather x1, waiting for transfers between devices, body(): reader_output_part = lax.all_gather(w_output, 'db', axis=0, tiled=True)  87.8 us
    all_gather x1, blocking collectives, body(): key_part = lax.all_gather(w_key, 'db', axis=0, tiled=True)  76.2 us
    all_gather x1, blocking collectives, body(): expand_part = lax.all_gather(w_expand, 'db', axis=0, tiled=True)  73.6 us
    all_gather x1, blocking collectives, body(): value_part = lax.all_gather(w_value, 'db', axis=0, tiled=True)  72.8 us
    all_gather x1, waiting for transfers between devices, body(): lax.all_gather(attended, 'seq', axis=1, tiled=True)  51.9 us
    gather x1, local copies, waits for them, and re-layouts, body(): outgoing = table[requests]  21.4 us
  transfers between devices with their start and end apart: 6, of which 3 were waited for; matrix products, arithmetic and copies ran while one was open for 10% of the time, Pallas kernels for 0%

profile of v1, /device:TPU:1, one launch (start us, length us, event | category | flops | bytes accessed | tf_op | source)
XLA Modules:
  0.0 786.6 jit_solution(4004170141466631833)
XLA Ops:
  6.5 1.9 stack.2
  8.4 19.2 %all-to-all-start.1 = ((bf16[64,32,256]{2,1,0:T(8,128)(2,1)}), bf16[64,32,256]{2,1,0:T(8,128)(2,1)S(1)}, u32[]{:S(2)}, u32[]{:S(2)}) async-start(bf16[64,32,256]{2,1,0:T(8,128)(2,1)} %stack.2), calls=%async_computation.1 | async-start | bytes 2097152 | tf_op jit(solution)/shard_map/all_to_all | solution.py:37
  27.9 115.7 %all-gather.2 = bf16[64,14,224]{2,1,0:T(8,128)(2,1)S(1)} all-gather(bf16[1,14,224]{2,1,0:T(8,128)(2,1)S(1)} %bitcast.55), channel_id=1, replica_groups=mesh['db'=64,'seq'=8] {'db'}, dimensions={0}, use_global_device_ids=true | all-gather | bytes 407680 | tf_op jit(solution)/shard_map/all_gather | solution.py:47
  143.8 73.6 %all-gather.1 = bf16[64,14,224]{2,1,0:T(8,128)(2,1)S(1)} all-gather(bf16[1,14,224]{2,1,0:T(8,128)(2,1)S(1)} %bitcast.56), channel_id=1, replica_groups=mesh['db'=64,'seq'=8] {'db'}, dimensions={0}, use_global_device_ids=true | all-gather | bytes 407680 | tf_op jit(solution)/shard_map/all_gather | solution.py:46
  217.4 1.0 reshape.307
  219.1 3.3 fusion.38
  222.5 72.8 %all-gather.4 = bf16[64,14,256]{2,1,0:T(8,128)(2,1)S(1)} all-gather(bf16[1,14,256]{2,1,0:T(8,128)(2,1)S(1)} %bitcast.57), channel_id=1, replica_groups=mesh['db'=64,'seq'=8] {'db'}, dimensions={0}, use_global_device_ids=true | all-gather | bytes 465920 | tf_op jit(solution)/shard_map/all_gather | solution.py:49
  295.3 76.2 %all-gather.3 = bf16[64,14,256]{2,1,0:T(8,128)(2,1)S(1)} all-gather(bf16[1,14,256]{2,1,0:T(8,128)(2,1)S(1)} %bitcast.58), channel_id=1, replica_groups=mesh['db'=64,'seq'=8] {'db'}, dimensions={0}, use_global_device_ids=true | all-gather | bytes 465920 | tf_op jit(solution)/shard_map/all_gather | solution.py:48
  372.0 1.6 convolution_convert_fusion.1
  373.7 21.4 %gather_fusion = bf16[2048,2,512]{2,1,0:T(2,128)(2,1)} fusion(bf16[128,2,512]{2,1,0:T(2,128)(2,1)S(1)} %reshape.274, s32[2048]{0:T(1024)S(1)} %broadcast_clamp_fusion), kind=kCustom, calls=%fused_computation | custom fusion | bytes 8396800 | tf_op jit(solution)/shard_map/gather | solution.py:62
  395.2 11.7 %all-to-all-start = ((bf16[64,32,2,512]{3,2,1,0:T(2,128)(2,1)}), bf16[64,32,2,512]{3,2,1,0:T(2,128)(2,1)}, u32[]{:S(2)}, u32[]{:S(2)}) async-start(bf16[64,32,2,512]{3,2,1,0:T(2,128)(2,1)} %bitcast.47), calls=%async_computation | async-start | bytes 8388608 | tf_op jit(solution)/shard_map/all_to_all | solution.py:63
  409.1 177.3 %all-gather.13.cloned.1.call-done = bf16[1,1024,2048]{2,1,0:T(8,128)(2,1)} async-done(((bf16[1,128,2048]{2,1,0:T(8,128)(2,1)}), bf16[1,1024,2048]{2,1,0:T(8,128)(2,1)}) %all-gather.13.cloned.1.call-update) | async-done | bytes 4194320 | tf_op jit(solution)/shard_map/all_gather | solution.py:40
  586.4 3.2 fusion
  589.9 1.3 fusion.11
  591.3 7.2 reshape.276
  598.5 20.1 %gather_fusion.1 = bf16[4096,512]{1,0:T(8,128)(2,1)} fusion(bf16[4096,512]{1,0:T(8,128)(2,1)} %reshape.276, s32[4096]{0:T(1024)S(1)} %fusion.75), kind=kCustom, calls=%fused_computation.1 | custom fusion | bytes 8404992 | tf_op jit(solution)/shard_map/gather | solution.py:74
  618.6 4.2 slice.29
  622.9 6.3 copy.31
  629.1 2.6 pad_slice_fusion
  632.4 0.9 fusion.9
  633.3 1.0 fusion.14
  635.8 87.8 %all-gather.11.cloned.1.call-done = bf16[2048,256]{1,0:T(8,128)(2,1)} async-done(((bf16[32,256]{1,0:T(8,128)(2,1)}), bf16[2048,256]{1,0:T(8,128)(2,1)}) %all-gather.11.cloned.1.call-update) | async-done | bytes 1048592 | tf_op jit(solution)/shard_map/all_gather | solution.py:39
  723.6 51.9 %all-gather.9.cloned.1.call-done = bf16[1024,2048]{1,0:T(8,128)(2,1)} async-done(((bf16[1024,256]{1,0:T(8,128)(2,1)}), bf16[1024,2048]{1,0:T(8,128)(2,1)}) %all-gather.9.cloned.1.call-update) | async-done | bytes 4194320 | tf_op jit(solution)/shard_map/all_gather | solution.py:102
  775.5 4.6 fusion.15
  (61 shorter events, 6.3 us)
Async XLA Ops:
  6.5 21.2 %copy-start.1 = (bf16[128,2,896]{2,1,0:T(2,128)(2,1)S(1)}, bf16[128,2,896]{2,1,0:T(2,128)(2,1)}, u32[]{:S(2)}) copy-start(bf16[128,2,896]{2,1,0:T(2,128)(2,1)} %param.15) | copy-start | bytes 1376260
  6.5 21.3 %copy-start.3 = (bf16[224,14]{0,1:T(8,128)(2,1)S(1)}, bf16[224,14]{0,1:T(8,128)(2,1)}, u32[]{:S(2)}) copy-start(bf16[224,14]{0,1:T(8,128)(2,1)} %param.18) | copy-start | bytes 18820
  8.4 135.4 %copy-start.4 = (bf16[14,224]{1,0:T(8,128)(2,1)S(1)}, bf16[14,224]{1,0:T(8,128)(2,1)}, u32[]{:S(2)}) copy-start(bf16[14,224]{1,0:T(8,128)(2,1)} %param.17) | copy-start | bytes 18820
  8.4 386.7 %all-to-all-start.1 = ((bf16[64,32,256]{2,1,0:T(8,128)(2,1)}), bf16[64,32,256]{2,1,0:T(8,128)(2,1)S(1)}, u32[]{:S(2)}, u32[]{:S(2)}) async-start(bf16[64,32,256]{2,1,0:T(8,128)(2,1)} %stack.2), calls=%async_computation.1 | async-start | bytes 2097152 | tf_op jit(solution)/shard_map/all_to_all | solution.py:37
  27.7 344.3 %all-reduce.4.cloned.1.call-start = ((), (), s32[]{:S(2)}) async-start(), calls=%async_computation.2 | async-start | bytes 1835008 | tf_op jit(solution)/shard_map/psum | solution.py:56
  27.9 191.2 %copy-start.10 = (f32[896]{0:T(1024)S(1)}, f32[896]{0:T(1024)}, u32[]{:S(2)}) copy-start(f32[896]{0:T(1024)} %param.16) | copy-start | bytes 10756
  219.1 3.4 copy-start.5
  219.1 76.2 %copy-start.6 = (bf16[14,256]{1,0:T(8,128)(2,1)S(1)}, bf16[14,256]{1,0:T(8,128)(2,1)}, u32[]{:S(2)}) copy-start(bf16[14,256]{1,0:T(8,128)(2,1)} %param.20) | copy-start | bytes 21508
  222.4 149.4 %copy-start.2 = (s32[64,8,4]{0,2,1:T(4,128)S(1)}, s32[64,8,4]{0,2,1:T(4,128)}, u32[]{:S(2)}) copy-start(s32[64,8,4]{0,2,1:T(4,128)} %param.23) | copy-start | bytes 24580
  395.2 13.4 %copy-start.7 = (s32[1,8,4]{1,2,0:T(4,128)S(1)}, s32[1,8,4]{1,2,0:T(4,128)}, u32[]{:S(2)}) copy-start(s32[1,8,4]{1,2,0:T(4,128)} %param.25) | copy-start | bytes 388
  395.2 13.6 %copy-start.8 = (s32[1,8,4]{1,2,0:T(4,128)S(1)}, s32[1,8,4]{1,2,0:T(4,128)}, u32[]{:S(2)}) copy-start(s32[1,8,4]{1,2,0:T(4,128)} %param.24) | copy-start | bytes 388
  395.2 196.1 %all-to-all-start = ((bf16[64,32,2,512]{3,2,1,0:T(2,128)(2,1)}), bf16[64,32,2,512]{3,2,1,0:T(2,128)(2,1)}, u32[]{:S(2)}, u32[]{:S(2)}) async-start(bf16[64,32,2,512]{3,2,1,0:T(2,128)(2,1)} %bitcast.47), calls=%async_computation | async-start | bytes 8388608 | tf_op jit(solution)/shard_map/all_to_all | solution.py:63
  406.8 179.6 %all-gather.13.cloned.1.call-start = ((), (), s32[]{:S(2)}) async-start(), calls=%async_computation.5 | async-start | bytes 4718592 | tf_op jit(solution)/shard_map/all_gather | solution.py:40
  407.6 316.0 %all-gather.11.cloned.1.call-start = ((), (), s32[]{:S(2)}) async-start(), calls=%async_computation.4 | async-start | bytes 1064960 | tf_op jit(solution)/shard_map/all_gather | solution.py:39
  408.3 367.1 %all-gather.9.cloned.1.call-start = ((), (), s32[]{:S(2)}) async-start(), calls=%async_computation.3 | async-start | bytes 4718592 | tf_op jit(solution)/shard_map/all_gather | solution.py:102
  409.1 180.5 %copy-start.9 = (f32[2048]{0:T(1024)S(1)}, f32[2048]{0:T(1024)}, u32[]{:S(2)}) copy-start(f32[2048]{0:T(1024)} %param.14) | copy-start | bytes 24580
  586.4 3.4 copy-start
Sparse Core Ops, SparseCore 0:
  222.6 124.5 all-reduce.3
  409.8 176.5 all-gather.12
  589.4 134.1 all-gather.10
  725.6 49.8 all-gather.8
